TPU v7x, 32 devices: a whole 2x2x4 slice. The times are simulated.
32 devices in a mesh: island: 8 (over z, x), fsdp: 4 (over y, core).
Axes of the slice: x: 2, y: 2, z: 4, core: 2. Of those that a mesh axis runs over, the one named last changes fastest.
Arguments:
- local_weights: bfloat16 [8, 4096, 512], P('island', 'fsdp'), may hold values from -6 to 6
- adam_first: bfloat16 [8, 4096, 512], P('island', 'fsdp'), may hold values from -6 to 6
- adam_second: bfloat16 [8, 4096, 512], P('island', 'fsdp'), may hold values from 0.5 to 4
- global_weights: float32 [4096, 512], P('fsdp'), may hold values from -6 to 6
- outer_momentum: float32 [4096, 512], P('fsdp'), may hold values from -3 to 3
- inputs: bfloat16 [8, 512, 4096], P('island', 'fsdp'), may hold values from -6 to 6
- key_cotangent: bfloat16 [8, 512, 512], P('island', 'fsdp'), may hold values from -24 to 24
Outputs:
- new_local: bfloat16 [8, 4096, 512], P('island', 'fsdp')
- new_first: bfloat16 [8, 4096, 512], P('island', 'fsdp')
- new_second: bfloat16 [8, 4096, 512], P('island', 'fsdp')
- new_global: float32 [4096, 512], P('fsdp')
- new_momentum: float32 [4096, 512], P('fsdp')
All inputs are finite; a program needn't handle non-finite values.
Results may differ from a plain program's by a relative error of at most 0.0065.
Values may be sent and summed in bfloat16 or wider, within the bound.
A program may use at most 64 MiB of HBM per device.

v0:
```python
import jax
import jax.numpy as jnp
from jax import lax
from jax.sharding import PartitionSpec as P

HEAD_DIM = 128
beta_one = 0.9
beta_two = 0.95
inner_rate = 0.02
weight_decay = 0.1
adam_epsilon = 1e-08
norm_epsilon = 1e-06
outer_rate = 0.7
outer_beta = 0.9
merge_weight = 0.5


def key_backward(keys, upstream):
    heads = keys.shape[1] // HEAD_DIM
    shaped = keys.reshape(keys.shape[0], heads, HEAD_DIM)
    cotan_heads = upstream.reshape(keys.shape[0], heads, HEAD_DIM)
    squares = jnp.mean(shaped * shaped, axis=-1, keepdims=True)
    inverse = lax.rsqrt(squares + norm_epsilon)
    normed = shaped * inverse
    projected = jnp.mean(cotan_heads * normed, axis=-1, keepdims=True)
    return (inverse * (cotan_heads - normed * projected)).reshape(keys.shape)


def local(
    local_weights, adam_first, adam_second, global_weights, outer_momentum, inputs, key_cotangent
):
    weights = local_weights[0]
    tokens = inputs[0]
    upstream = key_cotangent[0].astype(jnp.float32)
    scale = float(tokens.shape[1]) ** (-0.5)
    islands = lax.axis_size("island")
    summed = lax.psum(weights.astype(jnp.float32), "island")
    outer_grad = global_weights - summed / islands
    new_momentum = outer_beta * outer_momentum + outer_grad
    new_global = global_weights - outer_rate * (outer_grad + outer_beta * new_momentum)
    columns = tokens
    keys = (
        jnp.dot(
            columns,
            lax.all_gather(weights, "fsdp", axis=0, tiled=True),
            preferred_element_type=jnp.float32,
        )
        * scale
    )
    key_grad = (key_backward(keys, upstream) * scale).astype(jnp.bfloat16)
    columns = tokens
    gradient = lax.psum_scatter(
        lax.dot_general(
            columns, key_grad, (((0,), (0,)), ((), ())), preferred_element_type=jnp.float32
        ).astype(jnp.bfloat16),
        "fsdp",
        scatter_dimension=0,
        tiled=True,
    ).astype(jnp.float32)
    first_new = beta_one * adam_first[0].astype(jnp.float32) + (1.0 - beta_one) * gradient
    second_new = (
        beta_two * adam_second[0].astype(jnp.float32) + (1.0 - beta_two) * gradient * gradient
    )
    current = weights.astype(jnp.float32)
    inner = current - inner_rate * (
        first_new / (jnp.sqrt(second_new) + adam_epsilon) + weight_decay * current
    )
    merged = merge_weight * inner + (1.0 - merge_weight) * new_global
    return (
        merged.astype(jnp.bfloat16)[None],
        first_new.astype(jnp.bfloat16)[None],
        second_new.astype(jnp.bfloat16)[None],
        new_global,
        new_momentum,
    )


def solution(mesh):
    placed = (
        P("island", "fsdp", None),
        P("island", "fsdp", None),
        P("island", "fsdp", None),
        P("fsdp", None),
        P("fsdp", None),
        P("island", "fsdp", None),
        P("island", "fsdp", None),
    )
    return jax.shard_map(
        local,
        mesh=mesh,
        in_specs=placed,
        out_specs=(
            P("island", "fsdp", None),
            P("island", "fsdp", None),
            P("island", "fsdp", None),
            P("fsdp", None),
            P("fsdp", None),
        ),
        check_vma=False,
    )
```

profile of v0, /device:TPU:0, one launch (start us, length us, event | category | flops | bytes accessed | tf_op | source)
XLA Modules:
  0.0 142.2 jit_solution(9254017359627056663)
XLA Ops:
  8.0 0.0 copy-start
  8.0 0.0 all-gather.3.cloned.1.call-start
  8.1 0.7 all-gather.3.cloned.1.call-update
  8.7 0.0 all-reduce.2.cloned.1.call-start
  8.8 1.5 %copy.12 = bf16[1,1024,512]{1,2,0:T(8,128)(2,1)S(1)} copy(bf16[1,1024,512]{2,1,0:T(8,128)(2,1)} %param.7) | data formatting | bytes 2097152 | tf_op args[0]
  10.3 0.0 copy-start.3
  10.3 1.6 %bitcast_convert_fusion = f32[1024,512]{0,1:T(8,128)} fusion(bf16[1,1024,512]{1,2,0:T(8,128)(2,1)S(1)} %copy.12), kind=kLoop, calls=%fused_computation.17 | loop fusion | flops 524288 | bytes 3145728 | tf_op jit(solution)/shard_map/convert_element_type | solution.py:64
  11.9 0.0 all-reduce.2.cloned.1.call-update
  11.9 0.0 reduce-scatter.2.cloned.1.call-start
  12.0 0.1 reshape.52
  12.1 35.5 %all-gather.3.cloned.1.call-done = bf16[1,4096,512]{2,1,0:T(8,128)(2,1)} async-done(((bf16[1,1024,512]{2,1,0:T(8,128)(2,1)}), bf16[1,4096,512]{2,1,0:T(8,128)(2,1)}) %all-gather.3.cloned.1.call-update) | async-done | bytes 4194320 | tf_op jit(solution)/shard_map/all_gather | solution.py:45
  47.6 0.0 copy-done
  47.6 2.9 %fusion.7 = f32[128,512]{1,0:T(8,128)S(1)} fusion(bf16[1,4096,512]{2,1,0:T(8,128)(2,1)} %all-gather.3.cloned.1.call-done, bf16[1,128,4096]{2,1,0:T(8,128)(2,1)S(1)} %copy-done), kind=kOutput, calls=%fused_computation.14 | convolution fusion | flops 536936448 | bytes 5505024 | tf_op jit(solution)/shard_map/dot_general | solution.py:43
  50.5 0.1 reshape.50
  50.6 0.2 multiply_reduce_fusion.1
  50.8 0.4 multiply_reduce_fusion
  51.2 0.2 mul.112
  51.4 0.2 mul.107
  51.6 3.3 %fusion = bf16[4096,512]{0,1:T(8,128)(2,1)} fusion(bf16[1,128,4096]{2,1,0:T(8,128)(2,1)S(1)} %copy-done, f32[16,8,4,128]{3,2,1,0:T(4,128)S(1)} %bitcast.65, f32[128,512]{1,0:T(8,128)S(1)} %fusion.7, f32[16,8,4,128]{3,2,1,0:T(4,128)S(1)} %bitcast.66, bf16[1,128,512]{2,1,0:T(8,128)(2,1)S(1)} %copy-done.3), kind=kOutput, calls=%fused_computation.1 | convolution fusion | flops 539426816 | bytes 6160384 | tf_op jit(solution)/shard_map/dot_general | solution.py:53
  54.9 0.0 reduce-scatter.2.cloned.1.call-update
  54.9 2.9 %copy.16 = f32[1024,512]{0,1:T(8,128)} copy(f32[1024,512]{1,0:T(8,128)} %param.11) | data formatting | bytes 4194304 | tf_op args[4]
  57.8 2.9 %copy.17 = f32[1024,512]{0,1:T(8,128)} copy(f32[1024,512]{1,0:T(8,128)} %param.10) | data formatting | bytes 4194304 | tf_op args[3]
  60.7 1.5 %copy.13 = bf16[1,1024,512]{1,2,0:T(8,128)(2,1)S(1)} copy(bf16[1,1024,512]{2,1,0:T(8,128)(2,1)} %param.8) | data formatting | bytes 2097152 | tf_op args[1]
  62.3 2.5 %copy.14 = bf16[1,1024,512]{1,2,0:T(8,128)(2,1)} copy(bf16[1,1024,512]{2,1,0:T(8,128)(2,1)} %param.9) | data formatting | bytes 2097152 | tf_op args[2]
  64.8 52.7 %all-reduce.2.cloned.1.call-done = f32[1024,512]{0,1:T(8,128)} async-done(((f32[1024,512]{0,1:T(8,128)}), f32[1024,512]{0,1:T(8,128)}) %all-reduce.2.cloned.1.call-update) | async-done | bytes 2097168 | tf_op jit(solution)/shard_map/psum | solution.py:37
  117.5 6.4 %fusion.14 = (bf16[1,1024,512]{1,2,0:T(8,128)(2,1)}, f32[1024,512]{0,1:T(8,128)}, f32[1024,512]{0,1:T(8,128)}, bf16[1,1024,512]{1,2,0:T(8,128)(2,1)}, bf16[1,1024,512]{1,2,0:T(8,128)(2,1)}) fusion(bf16[1,1024,512]{1,2,0:T(8,128)(2,1)} %copy.14, bf16[1024,512]{0,1:T(8,128)(2,1)} %reduce-scatter.2.cloned.1.call-done, bf16[1,1024,512]{1,2,0:T(8,128)(2,1)S(1)} %copy.13, ...), kind=kLoop, calls=%fused_computation.20 | loop fusion | flops 15728640 | bytes 17825792 | tf_op jit(solution)/shard_map/broadcast_in_dim | solution.py:70
  123.9 2.9 %copy.21 = f32[1024,512]{1,0:T(8,128)} copy(f32[1024,512]{0,1:T(8,128)} %get-tuple-element.11) | data formatting | bytes 4194304
  126.8 2.9 %copy.22 = f32[1024,512]{1,0:T(8,128)} copy(f32[1024,512]{0,1:T(8,128)} %get-tuple-element.12) | data formatting | bytes 4194304
  129.7 2.4 %copy.18 = bf16[1,1024,512]{2,1,0:T(8,128)(2,1)} copy(bf16[1,1024,512]{1,2,0:T(8,128)(2,1)} %get-tuple-element.10) | data formatting | bytes 2097152
  132.1 1.3 copy.19
  133.4 0.0 copy-done.1
  133.4 1.3 copy.20
  (7 shorter events, 0.0 us)
Async XLA Ops:
  8.0 39.6 %copy-start = (bf16[1,128,4096]{2,1,0:T(8,128)(2,1)S(1)}, bf16[1,128,4096]{2,1,0:T(8,128)(2,1)}, u32[]{:S(2)}) copy-start(bf16[1,128,4096]{2,1,0:T(8,128)(2,1)} %param.12) | copy-start | bytes 3145732
  8.0 39.6 %all-gather.3.cloned.1.call-start = ((), (), s32[]{:S(2)}) async-start(), calls=%async_computation.3 | async-start | bytes 5242880 | tf_op jit(solution)/shard_map/all_gather | solution.py:45
  8.7 108.8 %all-reduce.2.cloned.1.call-start = ((), (), s32[]{:S(2)}) async-start(), calls=%async_computation.2 | async-start | bytes 4194304 | tf_op jit(solution)/shard_map/psum | solution.py:37
  10.3 1.7 %copy-start.3 = (bf16[1,128,512]{2,1,0:T(8,128)(2,1)S(1)}, bf16[1,128,512]{2,1,0:T(8,128)(2,1)}, u32[]{:S(2)}) copy-start(bf16[1,128,512]{2,1,0:T(8,128)(2,1)} %param.13) | copy-start | bytes 393220
  11.9 105.6 %reduce-scatter.2.cloned.1.call-start = ((), (), s32[]{:S(2)}) async-start(), calls=%async_computation.1 | async-start | bytes 5242880 | tf_op jit(solution)/shard_map/reduce_scatter | solution.py:52
  129.7 2.4 %copy-start.2 = (bf16[1,1024,512]{1,2,0:T(8,128)(2,1)S(1)}, bf16[1,1024,512]{1,2,0:T(8,128)(2,1)}, u32[]{:S(2)}) copy-start(bf16[1,1024,512]{1,2,0:T(8,128)(2,1)} %get-tuple-element.14) | copy-start | bytes 3145732
  129.7 3.7 %copy-start.1 = (bf16[1,1024,512]{1,2,0:T(8,128)(2,1)S(1)}, bf16[1,1024,512]{1,2,0:T(8,128)(2,1)}, u32[]{:S(2)}) copy-start(bf16[1,1024,512]{1,2,0:T(8,128)(2,1)} %get-tuple-element.13) | copy-start | bytes 3145732
Sparse Core Ops, SparseCore 0:
  10.4 37.1 all-gather.2
  55.0 44.4 reduce-scatter.1
Sparse Core Ops, SparseCore 1:
  12.8 104.6 all-reduce.1
where the time goes:
time: 143 us; the launch traced here: 142 us
  waiting for transfers between devices  88.9 us (62%)
  local copies, waits for them, and re-layouts  22.8 us (16%)
  between operations  15.6 us (11%)
  other arithmetic  8.62 us (6%)
  matrix products  6.16 us (4%)
    psum x1, waiting for transfers between devices, local(): summed = lax.psum(weights.astype(jnp.float32), 'island')  52.7 us
    all_gather x1, waiting for transfers between devices, local(): lax.all_gather(weights, 'fsdp', axis=0, tiled=True)  35.5 us
    unnamed x18, local copies, waits for them, and re-layouts  22.2 us
    broadcast_in_dim x1, other arithmetic, local(): merged.astype(jnp.bfloat16)[None]  6.43 us
    dot_general x1, matrix products, local(): lax.dot_general(columns, key_grad, (((0,), (0,)), ((), ())), preferred_el...  3.25 us
    dot_general x1, matrix products, local(): jnp.dot(columns, lax.all_gather(weights, 'fsdp', axis=0, tiled=True), pre...  2.9 us
  transfers between devices with their start and end apart: 3, of which 2 were waited for; matrix products, arithmetic and copies ran while one was open for 14% of the time, Pallas kernels for 0%

commit v1 on v0

--- a/solution.py
+++ b/solution.py
@@ -34,7 +34,7 @@
     upstream = key_cotangent[0].astype(jnp.float32)
     scale = float(tokens.shape[1]) ** (-0.5)
     islands = lax.axis_size("island")
-    summed = lax.psum(weights.astype(jnp.float32), "island")
+    summed = jnp.sum(lax.all_gather(weights.astype(jnp.float32), "island"), axis=0)
     outer_grad = global_weights - summed / islands
     new_momentum = outer_beta * outer_momentum + outer_grad
     new_global = global_weights - outer_rate * (outer_grad + outer_beta * new_momentum)

time: 143 us -> 346 us (2.42)
  waiting for transfers between devices: 88.9 us -> 281 us
  other arithmetic: 8.62 us -> 16.5 us
  local copies, waits for them, and re-layouts: 22.8 us -> 27.7 us
    all_gather x0 -> x1, waiting for transfers between devices: none -> 212 us  [local(): lax.all_gather(weights.astype(jnp.float32), 'island')]
    psum x1 -> x0, waiting for transfers between devices: 52.7 us -> none  [local(): summed = lax.psum(weights.astype(jnp.float32), 'island')]
    reduce_scatter x1, waiting for transfers between devices: 0.01 us -> 32.6 us  [local(): lax.psum_scatter(lax.dot_general(columns, key_grad, (((0,), (0,)), ((), (...]
    reduce_sum x0 -> x1, other arithmetic: none -> 9.45 us  [local(): jnp.sum(lax.all_gather(weights.astype(jnp.float32), 'island'), axis=0)]
  transfers between devices with their start and end apart: 3 -> 3, of which waited for: 2 -> 3; matrix products, arithmetic and copies ran while one was open for 14% -> 10% of each run, Pallas kernels for 0% -> 0%
where the time goes in v1:
time: 346 us; the launch traced here: 345 us
  waiting for transfers between devices  281 us (81%)
  local copies, waits for them, and re-layouts  27.7 us (8%)
  other arithmetic  16.5 us (5%)
  between operations  13.8 us (4%)
  matrix products  6.15 us (2%)
    all_gather x1, waiting for transfers between devices, local(): lax.all_gather(weights.astype(jnp.float32), 'island')  212 us
    all_gather x1, waiting for transfers between devices, local(): lax.all_gather(weights, 'fsdp', axis=0, tiled=True)  35.5 us
    reduce_scatter x1, waiting for transfers between devices, local(): lax.psum_scatter(lax.dot_general(columns, key_grad, (((0,), (0,)), ((), (...  32.6 us
    unnamed x18, local copies, waits for them, and re-layouts  22.4 us
    reduce_sum x1, other arithmetic, local(): jnp.sum(lax.all_gather(weights.astype(jnp.float32), 'island'), axis=0)  9.45 us
  transfers between devices with their start and end apart: 3, of which 3 were waited for; matrix products, arithmetic and copies ran while one was open for 10% of the time, Pallas kernels for 0%

profile of v1, /device:TPU:0, one launch (start us, length us, event | category | flops | bytes accessed | tf_op | source)
XLA Modules:
  0.0 345.2 jit_solution(1921339373634203878)
XLA Ops:
  7.2 0.0 copy-start
  7.2 0.0 all-gather.6.cloned.1.call-start
  7.2 0.7 all-gather.6.cloned.1.call-update
  7.9 0.0 all-gather.4.cloned.1.call-start
  8.0 1.5 copy.35
  9.5 1.6 copy.38
  11.1 0.0 all-gather.4.cloned.1.call-update
  11.1 0.0 reduce-scatter.2.cloned.1.call-start
  11.2 0.1 reshape.52
  11.3 35.5 %all-gather.6.cloned.1.call-done = bf16[1,4096,512]{2,1,0:T(8,128)(2,1)} async-done(((bf16[1,1024,512]{2,1,0:T(8,128)(2,1)}), bf16[1,4096,512]{2,1,0:T(8,128)(2,1)}) %all-gather.6.cloned.1.call-update) | async-done | bytes 4194320 | tf_op jit(solution)/shard_map/all_gather | solution.py:45
  46.8 2.9 fusion.12
  49.7 0.1 reshape.50
  49.8 0.2 multiply_reduce_fusion.1
  50.0 0.4 multiply_reduce_fusion
  50.4 0.2 mul.112
  50.6 0.2 mul.107
  50.8 3.2 fusion
  54.1 0.0 reduce-scatter.2.cloned.1.call-update
  54.1 2.9 copy.41
  57.0 3.2 copy.42
  60.2 1.6 copy.36
  61.9 2.3 copy.37
  64.1 212.1 %all-gather.4.cloned.1.call-done = f32[8,1024,512]{2,1,0:T(8,128)} async-done(((f32[1,1024,512]{2,1,0:T(8,128)}), f32[8,1024,512]{2,1,0:T(8,128)}) %all-gather.4.cloned.1.call-update) | async-done | bytes 16777232 | tf_op jit(solution)/shard_map/all_gather | solution.py:37
  276.2 9.4 %reduce_sum.29 = f32[1024,512]{1,0:T(8,128)} reduce(f32[8,1024,512]{2,1,0:T(8,128)} %all-gather.4.cloned.1.call-done, f32[]{:T(128)} %constant.5.clone.1), dimensions={0}, to_apply=%region_3.0 | reduce | flops 3670016 | bytes 18874372 | tf_op jit(solution)/shard_map/reduce_sum | solution.py:37
  285.6 3.1 copy.39
  288.8 32.6 %reduce-scatter.2.cloned.1.call-done = bf16[1024,512]{0,1:T(8,128)(2,1)} async-done(((bf16[4096,512]{0,1:T(8,128)(2,1)}), bf16[1024,512]{0,1:T(8,128)(2,1)}) %reduce-scatter.2.cloned.1.call-update) | async-done | bytes 1048592 | tf_op jit(solution)/shard_map/reduce_scatter | solution.py:52
  321.4 6.4 %fusion.19 = (bf16[1,1024,512]{1,2,0:T(8,128)(2,1)}, f32[1024,512]{0,1:T(8,128)}, f32[1024,512]{0,1:T(8,128)}, bf16[1,1024,512]{1,2,0:T(8,128)(2,1)}, bf16[1,1024,512]{1,2,0:T(8,128)(2,1)}) fusion(bf16[1,1024,512]{1,2,0:T(8,128)(2,1)} %copy.37, bf16[1024,512]{0,1:T(8,128)(2,1)} %reduce-scatter.2.cloned.1.call-done, bf16[1,1024,512]{1,2,0:T(8,128)(2,1)S(1)} %copy.36, ...), kind=kLoop, calls=%fused_computation.25 | loop fusion | flops 15728640 | bytes 17825792 | tf_op jit(solution)/shard_map/broadcast_in_dim | solution.py:70
  327.8 2.9 copy.46
  330.7 2.9 copy.47
  333.6 2.4 copy.43
  336.0 1.3 copy.44
  337.3 1.3 copy.45
  (9 shorter events, 0.0 us)
Async XLA Ops:
  7.2 39.6 %copy-start = (bf16[1,128,4096]{2,1,0:T(8,128)(2,1)S(1)}, bf16[1,128,4096]{2,1,0:T(8,128)(2,1)}, u32[]{:S(2)}) copy-start(bf16[1,128,4096]{2,1,0:T(8,128)(2,1)} %param.12) | copy-start | bytes 3145732
  7.2 39.6 %all-gather.6.cloned.1.call-start = ((), (), s32[]{:S(2)}) async-start(), calls=%async_computation.3 | async-start | bytes 5242880 | tf_op jit(solution)/shard_map/all_gather | solution.py:45
  7.9 268.3 %all-gather.4.cloned.1.call-start = ((), (), s32[]{:S(2)}) async-start(), calls=%async_computation.2 | async-start | bytes 18874368 | tf_op jit(solution)/shard_map/all_gather | solution.py:37
  9.5 1.7 copy-start.3
  11.1 310.3 %reduce-scatter.2.cloned.1.call-start = ((), (), s32[]{:S(2)}) async-start(), calls=%async_computation.1 | async-start | bytes 5242880 | tf_op jit(solution)/shard_map/reduce_scatter | solution.py:52
  333.6 2.4 copy-start.2
  333.6 3.7 %copy-start.1 = (bf16[1,1024,512]{1,2,0:T(8,128)(2,1)S(1)}, bf16[1,1024,512]{1,2,0:T(8,128)(2,1)}, u32[]{:S(2)}) copy-start(bf16[1,1024,512]{1,2,0:T(8,128)(2,1)} %get-tuple-element.23) | copy-start | bytes 3145732
Sparse Core Ops, SparseCore 0:
  9.5 37.1 all-gather.5
  48.9 227.2 all-gather.3
  278.7 42.5 reduce-scatter.1
